TPU v7x, 32 devices: a whole 2x2x4 slice. The times are simulated.
32 devices in a mesh: seg: 4 (over z), grp: 4 (over y, x), pair: 2 (over core).
Axes of the slice: x: 2, y: 2, z: 4, core: 2. Of those that a mesh axis runs over, the one named last changes fastest.
Arguments:
- observations: float32 [128, 256], P(('grp', 'seg')), may hold values from -6 to 6
- masks: int32 [128, 256], P(('grp', 'seg')), may hold values 0 or 1
- gains: float32 [256], replicated, may hold values from 0.05 to 0.5
- transition: float32 [256, 256], replicated, may hold values from -1 to 1, as said below
- smoother_scale: float32 [256], replicated, may hold values from 0.995 to 0.9999
- initial_mean: float32 [256], replicated, may hold values from -8 to 8
Outputs:
- filtered: float32 [128, 256], P(('grp', 'seg'), 'pair')
- smoothed: float32 [128, 256], P(('grp', 'seg'), 'pair')
Inputs may be any that keep to these rules, and one draw needn't show every extreme that they name: Each column of transition is a unit vector scaled by a factor in (0, 1); the columns are orthogonal.
All inputs are finite; a program needn't handle non-finite values. No bound on the sum of `masks` on one device may be relied on, other than what follows from the above.
Results may differ from a plain program's by a relative error of at most 0.0003.
Values sent between devices are 32-bit elements; how exact they have to be, the bound alone decides.
No kernel may reach another device: no remote copies, remote signals or barrier semaphores. Data moves between devices by JAX's collectives and lax.ppermute only.
A program may use at most 64 MiB of HBM per device.

v0:
```python
import jax
import jax.numpy as jnp
from jax import lax
from jax.sharding import PartitionSpec as P


def entering(x, axis, combine, identity, reverse):
    size, here = (lax.axis_size(axis), lax.axis_index(axis))
    everything = jax.tree.map(lambda part: lax.all_gather(part, axis), x)
    start = jax.tree.map(
        lambda part, zero: jnp.broadcast_to(jnp.asarray(zero, part.dtype), part.shape), x, identity
    )

    def turn(k, before):
        at = size - 1 - k if reverse else k
        reached = at > here if reverse else at < here
        new = combine(before, jax.tree.map(lambda part: part[at], everything))
        return jax.tree.map(lambda a, b: jnp.where(reached, a, b), new, before)

    return lax.fori_loop(0, size, turn, start)


def spread(value, axis, source):
    kept = jnp.where(lax.axis_index(axis) == source, value, 0).astype(value.dtype)
    return lax.psum(kept, axis)


def shifted(value, axis, steps):
    count = lax.axis_size(axis)
    initial, last = (max(0, -steps), min(count, count - steps))
    return lax.ppermute(value, axis, [(source, source + steps) for source in range(initial, last)])


def compose(earlier, later_elem):
    highest = lax.Precision.HIGHEST
    matrix = jnp.dot(later_elem[0], earlier[0], precision=highest)
    offset = jnp.dot(later_elem[0], earlier[1], precision=highest) + later_elem[1]
    return (matrix, offset)


def shards(observations, masks, gains, transition, smoother_scale, initial_mean):
    highest = lax.Precision.HIGHEST
    state_width = transition.shape[0]
    day_count = observations.shape[0]
    observed = masks.astype(jnp.float32) * gains[None, :]
    retain = 1.0 - observed
    forcing = observed * observations
    smoother_gain = smoother_scale[:, None] * transition.T
    half_cols = state_width // lax.axis_size("pair")
    col_start = lax.axis_index("pair") * half_cols

    def forward_advance(position, product):
        scaled = jnp.dot(transition, product, precision=highest)
        return lax.dynamic_index_in_dim(retain, position, 0, False)[:, None] * scaled

    forward_half = lax.fori_loop(
        1,
        day_count,
        forward_advance,
        retain[0][:, None] * lax.dynamic_slice_in_dim(transition, col_start, half_cols, 1),
    )

    def gain_advance(position, product):
        return jnp.dot(smoother_gain, product, precision=highest)

    power_half = lax.fori_loop(
        1, day_count, gain_advance, lax.dynamic_slice_in_dim(smoother_gain, col_start, half_cols, 1)
    )
    fwd_matrix, gain_matrix = (
        lax.all_gather(forward_half, "pair", axis=1, tiled=True),
        lax.all_gather(power_half, "pair", axis=1, tiled=True),
    )

    def forward_run(mean_start):

        def forward_step(mean_prev, row_pair):
            retain_row, forcing_row = row_pair
            mean_next = retain_row * jnp.dot(transition, mean_prev, precision=highest) + forcing_row
            return (mean_next, mean_next)

        return lax.scan(forward_step, mean_start, (retain, forcing))

    def backward_run(smooth_end, means):

        def backward_step(smooth_next, mean_here):
            predicted = jnp.dot(transition, mean_here, precision=highest)
            smooth_here = mean_here + jnp.dot(
                smoother_gain, smooth_next - predicted, precision=highest
            )
            return (smooth_here, smooth_here)

        return lax.scan(backward_step, smooth_end, means, reverse=True)

    zeros_vec = jnp.zeros((state_width,), jnp.float32)
    identity = (jnp.eye(state_width, dtype=jnp.float32), zeros_vec)
    seg_count = lax.axis_size("seg")
    seg_index = lax.axis_index("seg")
    grp_count = lax.axis_size("grp")
    grp_index = lax.axis_index("grp")
    fwd_offset, unused = forward_run(zeros_vec)
    own_forward = (fwd_matrix, fwd_offset)
    before = entering(own_forward, "seg", compose, identity, False)
    through = compose(before, own_forward)
    group_total = (
        spread(through[0], "seg", seg_count - 1),
        spread(through[1], "seg", seg_count - 1),
    )
    entry_mean = initial_mean
    for rounds in range(1, grp_count):
        leaving = jnp.dot(group_total[0], entry_mean, precision=highest) + group_total[1]
        arrived = shifted(leaving, "grp", 1)
        entry_mean = jnp.where(grp_index == rounds, arrived, entry_mean)
    start_mean = jnp.dot(before[0], entry_mean, precision=highest) + before[1]
    last_mean, filtered = forward_run(start_mean)
    back_offset, unused_two = backward_run(zeros_vec, filtered)
    is_last = jnp.logical_and(seg_index == seg_count - 1, grp_index == grp_count - 1)
    boundary = jnp.dot(transition, last_mean, precision=highest)
    own_backward = (
        jnp.where(is_last, 0.0, gain_matrix),
        jnp.where(
            is_last, jnp.dot(gain_matrix, boundary, precision=highest) + back_offset, back_offset
        ),
    )
    behind = entering(own_backward, "seg", compose, identity, True)
    through_back = compose(behind, own_backward)
    back_total = (spread(through_back[0], "seg", 0), spread(through_back[1], "seg", 0))
    exit_smooth = zeros_vec
    for rounds in range(1, grp_count):
        leaving_back = jnp.dot(back_total[0], exit_smooth, precision=highest) + back_total[1]
        arrived_back = shifted(leaving_back, "grp", -1)
        exit_smooth = jnp.where(grp_index == grp_count - 1 - rounds, arrived_back, exit_smooth)
    smooth_end = jnp.dot(behind[0], exit_smooth, precision=highest) + behind[1]
    smooth_end = jnp.where(is_last, boundary, smooth_end)
    unused_three, smoothed = backward_run(smooth_end, filtered)
    out_cols = state_width // lax.axis_size("pair")
    out_start = lax.axis_index("pair") * out_cols
    filtered_part = lax.dynamic_slice_in_dim(filtered, out_start, out_cols, 1)
    smoothed_part = lax.dynamic_slice_in_dim(smoothed, out_start, out_cols, 1)
    return (filtered_part, smoothed_part)


def solution(mesh):
    return jax.shard_map(
        shards,
        mesh=mesh,
        in_specs=(P(("grp", "seg"), None), P(("grp", "seg"), None), P(), P(), P(), P()),
        out_specs=(P(("grp", "seg"), "pair"), P(("grp", "seg"), "pair")),
        check_vma=False,
    )
```

profile of v0, /device:TPU:0, one launch (start us, length us, event | category | flops | bytes accessed | tf_op | source)
XLA Modules:
  0.0 218.8 jit_solution(14768913008447524611)
XLA Ops:
  7.2 0.6 copy-done.8
  7.9 0.7 fusion.19
  8.6 1.0 dynamic-slice_multiply_fusion
  9.6 3.1 %while.113 = (s32[]{:T(128)}, f32[256,128]{1,0:T(8,128)S(1)}, f32[8,256]{1,0:T(8,128)S(1)}, f32[256,256]{1,0:T(8,128)S(1)}, s32[]{:T(128)}, /*index=5*/s32[]{:T(128)}, s32[]{:T(128)}) while((s32[]{:T(128)}, f32[256,128]{1,0:T(8,128)S(1)}, f32[8,256]{1,0:T(8,128)S(1)}, f32[256,256]{1,0:T(8,128)S(1)}, s32[]{:T(128)}, /*index=5*/s32[]{:T(128)}, ...), condition=%wide.region_1.2_spmd, body=%wide.region_0.1_spmd.sunk | while | flops 100696064 | bytes 789627 | solution.py:56
  10.1 0.4 convolution_multiply_fusion.2
  10.5 0.4 convolution_multiply_fusion.2
  11.4 0.4 convolution_multiply_fusion.2
  11.8 0.4 convolution_multiply_fusion.2
  12.3 0.4 convolution_multiply_fusion.2
  12.7 2.3 %all_gather.30 = f32[256,256]{1,0:T(8,128)} all-gather(f32[256,128]{1,0:T(8,128)S(1)} %get-tuple-element.679), channel_id=1, replica_groups=mesh['seg'=4,'grp'=4,'pair'=2] {'pair'}, dimensions={1}, use_global_device_ids=true | all-gather | bytes 393216 | tf_op jit(solution)/shard_map/all_gather | solution.py:70
  15.0 2.9 %while.117 = (s32[]{:T(128)}, f32[256]{0:T(256)S(1)}, f32[8,256]{1,0:T(8,128)S(1)}, f32[256,256]{1,0:T(8,128)S(1)}, f32[8,256]{1,0:T(8,128)S(1)}, /*index=5*/s32[]{:T(128)}, s32[]{:T(128)}) while((s32[]{:T(128)}, f32[256]{0:T(256)S(1)}, f32[8,256]{1,0:T(8,128)S(1)}, f32[256,256]{1,0:T(8,128)S(1)}, f32[8,256]{1,0:T(8,128)S(1)}, ...), condition=%wide.region_3.4_spmd.clone, body=%wide.region_2.3_spmd.clone.sunk | while | flops 787203 | bytes 274523 | solution.py:81
  18.0 12.5 %all-gather.4 = f32[4,1,256]{2,1,0:T(1,128)S(1)} all-gather(f32[1,1,256]{2,1,0:T(1,128)S(1)} %bitcast.253), channel_id=3, replica_groups=mesh['seg'=4,'grp'=4,'pair'=2] {'seg'}, dimensions={0}, use_global_device_ids=true | all-gather | bytes 5120 | tf_op jit(solution)/shard_map/all_gather | solution.py:9
  30.6 0.7 copy-done.1
  31.3 0.7 copy-done.9
  32.2 13.5 %all-gather.9.cloned.1.call-done = f32[1024,256]{1,0:T(8,128)} async-done(((f32[256,256]{1,0:T(8,128)}), f32[1024,256]{1,0:T(8,128)}) %all-gather.9.cloned.1.call-update) | async-done | bytes 1048592 | tf_op jit(solution)/shard_map/all_gather | solution.py:9
  45.7 10.8 %while.118 = (s32[]{:T(128)}, f32[256,256]{1,0:T(8,128)S(1)}, f32[256]{0:T(256)S(1)}, s32[]{:T(128)}, f32[4,256,256]{2,1,0:T(8,128)}, /*index=5*/f32[4,256]{1,0:T(4,128)S(1)}, s32[]{:T(128)}, s32[]{:T(128)}) while((s32[]{:T(128)}, f32[256,256]{1,0:T(8,128)S(1)}, f32[256]{0:T(256)S(1)}, s32[]{:T(128)}, f32[4,256,256]{2,1,0:T(8,128)}, ...), condition=%wide.region_5.6_spmd.clone, body=%wide.region_4.5_spmd.clone.sunk | while | flops 202179584 | bytes 1846383 | solution.py:20
  45.7 1.3 fusion.140
  47.1 1.3 convolution_select_fusion.6
  48.5 1.2 fusion.140
  49.8 1.3 convolution_select_fusion.6
  51.2 1.2 fusion.140
  52.5 1.3 convolution_select_fusion.6
  53.9 1.2 fusion.140
  55.2 1.3 convolution_select_fusion.6
  56.6 1.1 convolution_select_fusion.3
  58.1 10.2 %psum.29 = f32[256]{0:T(256)S(1)} all-reduce(f32[256]{0:T(256)S(1)} %add_select_fusion.5), channel_id=1, replica_groups=mesh['seg'=4,'grp'=4,'pair'=2] {'seg'}, use_global_device_ids=true, to_apply=%region_7.8 | all-reduce | flops 256 | bytes 2048 | tf_op jit(solution)/shard_map/psum | solution.py:25
  68.3 24.4 %all-reduce.3.cloned.1.call-done = f32[256,256]{1,0:T(8,128)} async-done(((f32[256,256]{1,0:T(8,128)}), f32[256,256]{1,0:T(8,128)}) %all-reduce.3.cloned.1.call-update) | async-done | bytes 262160 | tf_op jit(solution)/shard_map/psum | solution.py:25
  92.7 1.2 fusion.31
  94.0 3.4 %collective-permute-start = (f32[256]{0:T(256)S(1)}, f32[256]{0:T(256)S(1)}, u32[]{:S(2)}, u32[]{:S(2)}) collective-permute-start(f32[256]{0:T(256)S(1)} %add.218), channel_id=1, source_target_pairs={{0,2},{2,4},{4,6},{1,3},{3,5},{5,7},{8,10},{10,12},{12,14},{9,11},... | collective-permute-start | bytes 3080 | tf_op jit(solution)/shard_map/ppermute | solution.py:31
  97.4 2.9 %while.115 = (s32[]{:T(128)}, f32[256,128]{1,0:T(8,128)S(1)}, f32[256,256]{1,0:T(8,128)S(1)}, s32[]{:T(128)}) while((s32[]{:T(128)}, f32[256,128]{1,0:T(8,128)S(1)}, f32[256,256]{1,0:T(8,128)S(1)}, s32[]{:T(128)}) %tuple.227), condition=%wide.region_11.12_spmd, body=%wide.region_10.11_spmd.sunk | while | flops 100663296 | bytes 786485 | solution.py:66
  97.4 0.4 fusion.126
  97.8 0.4 fusion.126
  98.7 0.4 fusion.126
  99.5 0.4 fusion.126
  100.6 3.4 %collective-permute-start.1 = (f32[256]{0:T(256)S(1)}, f32[256]{0:T(256)S(1)}, u32[]{:S(2)}, u32[]{:S(2)}) collective-permute-start(f32[256]{0:T(256)S(1)} %add.219), channel_id=1, source_target_pairs={{0,2},{2,4},{4,6},{1,3},{3,5},{5,7},{8,10},{10,12},{12,14},{9,11},... | collective-permute-start | bytes 3080 | tf_op jit(solution)/shard_map/ppermute | solution.py:31
  104.1 2.0 all_gather.35
  106.3 3.5 %collective-permute-start.2 = (f32[256]{0:T(256)S(1)}, f32[256]{0:T(256)S(1)}, u32[]{:S(2)}, u32[]{:S(2)}) collective-permute-start(f32[256]{0:T(256)S(1)} %add.220), channel_id=1, source_target_pairs={{0,2},{2,4},{4,6},{1,3},{3,5},{5,7},{8,10},{10,12},{12,14},{9,11},... | collective-permute-start | bytes 3080 | tf_op jit(solution)/shard_map/ppermute | solution.py:31
  109.9 0.7 broadcast_select_fusion.3
  110.7 0.5 collective-permute-done.2
  111.5 3.2 %while.114 = (s32[]{:T(128)}, f32[256]{0:T(256)S(1)}, f32[8,256]{1,0:T(8,128)S(1)}, f32[8,256]{1,0:T(8,128)S(1)}, f32[256,256]{1,0:T(8,128)S(1)}, /*index=5*/f32[8,256]{1,0:T(8,128)S(1)}, s32[]{:T(128)}, s32[]{:T(128)}) while((s32[]{:T(128)}, f32[256]{0:T(256)S(1)}, f32[8,256]{1,0:T(8,128)S(1)}, f32[8,256]{1,0:T(8,128)S(1)}, ...), condition=%wide.region_9.10_spmd, body=%wide.region_8.9_spmd.sunk | while | flops 786946 | bytes 274525 | solution.py:81
  114.7 5.3 %while.119 = (s32[]{:T(128)}, f32[256]{0:T(256)S(1)}, f32[8,256]{1,0:T(8,128)S(1)}, f32[256,256]{1,0:T(8,128)S(1)}, f32[256,256]{1,0:T(8,128)S(1)}, /*index=5*/s32[]{:T(128)}, s32[]{:T(128)}, s32[]{:T(128)}) while((s32[]{:T(128)}, f32[256]{0:T(256)S(1)}, f32[8,256]{1,0:T(8,128)S(1)}, f32[256,256]{1,0:T(8,128)S(1)}, ...), condition=%wide.region_13.14_spmd.clone, body=%wide.region_12.13_spmd.clone.sunk | while | flops 1573636 | bytes 536687 | solution.py:92
  120.7 10.2 %all-gather.5 = f32[4,1,256]{2,1,0:T(1,128)S(1)} all-gather(f32[1,1,256]{2,1,0:T(1,128)S(1)} %bitcast.260), channel_id=5, replica_groups=mesh['seg'=4,'grp'=4,'pair'=2] {'seg'}, dimensions={0}, use_global_device_ids=true | all-gather | bytes 5120 | tf_op jit(solution)/shard_map/all_gather | solution.py:9
  130.9 7.8 %all-gather.11.cloned.1.call-done = f32[1024,256]{1,0:T(8,128)} async-done(((f32[256,256]{1,0:T(8,128)}), f32[1024,256]{1,0:T(8,128)}) %all-gather.11.cloned.1.call-update) | async-done | bytes 1048592 | tf_op jit(solution)/shard_map/all_gather | solution.py:9
  138.7 10.9 %while.120 = (s32[]{:T(128)}, f32[256,256]{1,0:T(8,128)S(1)}, f32[256]{0:T(256)S(1)}, s32[]{:T(128)}, f32[4,256,256]{2,1,0:T(8,128)}, /*index=5*/f32[4,256]{1,0:...) while((s32[]{:T(128)}, f32[256,256]{1,0:T(8,128)S(1)}, f32[256]{0:T(256)S(1)}, ...), condition=%wide.region_15.16_spmd.clone, body=%wide.region_14.15_spmd.clone.sunk | while | flops 202179584 | bytes 1845429 | solution.py:20
  138.7 1.3 fusion.151
  140.1 1.3 convolution_select_fusion.7
  141.5 1.2 fusion.151
  142.8 1.3 convolution_select_fusion.7
  144.2 1.2 fusion.151
  145.5 1.3 convolution_select_fusion.7
  146.9 1.2 fusion.151
  148.2 1.3 convolution_select_fusion.7
  149.6 1.1 convolution_select_fusion.2
  151.1 10.2 %psum.31 = f32[256]{0:T(256)S(1)} all-reduce(f32[256]{0:T(256)S(1)} %add_select_fusion.4), channel_id=1, replica_groups=mesh['seg'=4,'grp'=4,'pair'=2] {'seg'}, use_global_device_ids=true, to_apply=%region_17.18 | all-reduce | flops 256 | bytes 2048 | tf_op jit(solution)/shard_map/psum | solution.py:25
  161.3 24.7 %all-reduce.5.cloned.1.call-done = f32[256,256]{1,0:T(8,128)} async-done(((f32[256,256]{1,0:T(8,128)}), f32[256,256]{1,0:T(8,128)}) %all-reduce.5.cloned.1.call-update) | async-done | bytes 262160 | tf_op jit(solution)/shard_map/psum | solution.py:25
  185.9 1.3 fusion.23
  187.2 1.3 collective-permute-start.3
  188.6 4.2 %collective-permute-done.3 = f32[256]{0:T(256)S(1)} collective-permute-done((f32[256]{0:T(256)S(1)}, f32[256]{0:T(256)S(1)}, u32[]{:S(2)}, u32[]{:S(2)}) %collective-permute-start.3) | collective-permute-done | bytes 1056 | tf_op jit(solution)/shard_map/ppermute | solution.py:31
  193.0 1.3 collective-permute-start.4
  194.4 4.5 %collective-permute-done.4 = f32[256]{0:T(256)S(1)} collective-permute-done((f32[256]{0:T(256)S(1)}, f32[256]{0:T(256)S(1)}, u32[]{:S(2)}, u32[]{:S(2)}) %collective-permute-start.4) | collective-permute-done | bytes 1056 | tf_op jit(solution)/shard_map/ppermute | solution.py:31
  199.2 1.3 collective-permute-start.5
  200.5 5.1 %collective-permute-done.5 = f32[256]{0:T(256)S(1)} collective-permute-done((f32[256]{0:T(256)S(1)}, f32[256]{0:T(256)S(1)}, u32[]{:S(2)}, u32[]{:S(2)}) %collective-permute-start.5) | collective-permute-done | bytes 1056 | tf_op jit(solution)/shard_map/ppermute | solution.py:31
  205.9 5.8 %while.116 = (s32[]{:T(128)}, f32[256]{0:T(256)S(1)}, f32[8,256]{1,0:T(8,128)S(1)}, f32[8,256]{1,0:T(8,128)S(1)}, f32[256,256]{1,0:T(8,128)S(1)}, /*index=5*/f32...) while((s32[]{:T(128)}, f32[256]{0:T(256)S(1)}, f32[8,256]{1,0:T(8,128)S(1)}, f32[8,256]{1,0:T(8,128)S(1)}, ...), condition=%wide.region_19.20_spmd, body=%wide.region_18.19_spmd.sunk | while | flops 1573379 | bytes 538737 | solution.py:92
  211.7 0.6 constant_dynamic-slice_fusion.9
  (280 shorter events, 22.5 us)
Async XLA Ops:
  7.2 0.7 copy-start.8
  7.2 2.4 %copy-start = (f32[256,256]{1,0:T(8,128)S(1)}, f32[256,256]{1,0:T(8,128)}, u32[]{:S(2)}) copy-start(f32[256,256]{1,0:T(8,128)} %param.25) | copy-start | bytes 786436
  7.2 38.5 %all-gather.9.cloned.1.call-start = ((), (), s32[]{:S(2)}) async-start(), calls=%async_computation.2 | async-start | bytes 1310720 | tf_op jit(solution)/shard_map/all_gather | solution.py:9
  14.9 77.8 %all-reduce.3.cloned.1.call-start = ((), (), s32[]{:S(2)}) async-start(), calls=%async_computation | async-start | bytes 524288 | tf_op jit(solution)/shard_map/psum | solution.py:25
  30.6 0.7 copy-start.1
  31.3 0.7 copy-start.9
  32.1 13.6 %copy-start.3 = (f32[256,256]{1,0:T(8,128)S(1)}, f32[256,256]{1,0:T(8,128)}, u32[]{:S(2)}) copy-start(f32[256,256]{1,0:T(8,128)} %copy-done.1) | copy-start | bytes 786436
  45.7 10.9 %copy-start.5 = (f32[256,256]{1,0:T(8,128)S(1)}, f32[256,256]{1,0:T(8,128)}, u32[]{:S(2)}) copy-start(f32[256,256]{1,0:T(8,128)} %all_gather.30) | copy-start | bytes 786436
  57.7 81.0 %all-gather.11.cloned.1.call-start = ((), (), s32[]{:S(2)}) async-start(), calls=%async_computation.3 | async-start | bytes 1310720 | tf_op jit(solution)/shard_map/all_gather | solution.py:9
  68.3 24.4 %copy-start.10 = (f32[256]{0:T(256)S(1)}, f32[256]{0:T(256)}, u32[]{:S(2)}) copy-start(f32[256]{0:T(256)} %param.27) | copy-start | bytes 3076
  94.0 6.3 %collective-permute-start = (f32[256]{0:T(256)S(1)}, f32[256]{0:T(256)S(1)}, u32[]{:S(2)}, u32[]{:S(2)}) collective-permute-start(f32[256]{0:T(256)S(1)} %add.218), channel_id=1, source_target_pairs={{0,2},{2,4},{4,6},{1,3},{3,5},{5,7},{8,10},{10,12},{12,14},{9,11},... | collective-permute-start | bytes 3080 | tf_op jit(solution)/shard_map/ppermute | solution.py:31
  97.4 3.0 %copy-start.6 = (f32[256,256]{1,0:T(8,128)S(1)}, f32[256,256]{1,0:T(8,128)}, u32[]{:S(2)}) copy-start(f32[256,256]{1,0:T(8,128)} %all-reduce.3.cloned.1.call-done) | copy-start | bytes 786436
  100.6 5.4 %collective-permute-start.1 = (f32[256]{0:T(256)S(1)}, f32[256]{0:T(256)S(1)}, u32[]{:S(2)}, u32[]{:S(2)}) collective-permute-start(f32[256]{0:T(256)S(1)} %add.219), channel_id=1, source_target_pairs={{0,2},{2,4},{4,6},{1,3},{3,5},{5,7},{8,10},{10,12},{12,14},{9,11},... | collective-permute-start | bytes 3080 | tf_op jit(solution)/shard_map/ppermute | solution.py:31
  106.3 4.8 %collective-permute-start.2 = (f32[256]{0:T(256)S(1)}, f32[256]{0:T(256)S(1)}, u32[]{:S(2)}, u32[]{:S(2)}) collective-permute-start(f32[256]{0:T(256)S(1)} %add.220), channel_id=1, source_target_pairs={{0,2},{2,4},{4,6},{1,3},{3,5},{5,7},{8,10},{10,12},{12,14},{9,11},... | collective-permute-start | bytes 3080 | tf_op jit(solution)/shard_map/ppermute | solution.py:31
  110.6 75.3 %all-reduce.5.cloned.1.call-start = ((), (), s32[]{:S(2)}) async-start(), calls=%async_computation.1 | async-start | bytes 524288 | tf_op jit(solution)/shard_map/psum | solution.py:25
  120.0 18.7 %copy-start.2 = (f32[256,256]{1,0:T(8,128)S(1)}, f32[256,256]{1,0:T(8,128)}, u32[]{:S(2)}) copy-start(f32[256,256]{1,0:T(8,128)} %copy-done.1) | copy-start | bytes 786436
  138.7 10.9 %copy-start.4 = (f32[256,256]{1,0:T(8,128)S(1)}, f32[256,256]{1,0:T(8,128)}, u32[]{:S(2)}) copy-start(f32[256,256]{1,0:T(8,128)} %broadcast_select_fusion.3) | copy-start | bytes 786436
  185.9 6.8 %copy-start.7 = (f32[256,256]{1,0:T(8,128)S(1)}, f32[256,256]{1,0:T(8,128)}, u32[]{:S(2)}) copy-start(f32[256,256]{1,0:T(8,128)} %all-reduce.5.cloned.1.call-done) | copy-start | bytes 786436
  187.2 5.5 %collective-permute-start.3 = (f32[256]{0:T(256)S(1)}, f32[256]{0:T(256)S(1)}, u32[]{:S(2)}, u32[]{:S(2)}) collective-permute-start(f32[256]{0:T(256)S(1)} %add.224), channel_id=1, source_target_pairs={{2,0},{4,2},{6,4},{3,1},{5,3},{7,5},{10,8},{12,10},{14,12},{11,9},... | collective-permute-start | bytes 3080 | tf_op jit(solution)/shard_map/ppermute | solution.py:31
  193.0 5.9 %collective-permute-start.4 = (f32[256]{0:T(256)S(1)}, f32[256]{0:T(256)S(1)}, u32[]{:S(2)}, u32[]{:S(2)}) collective-permute-start(f32[256]{0:T(256)S(1)} %add.225), channel_id=1, source_target_pairs={{2,0},{4,2},{6,4},{3,1},{5,3},{7,5},{10,8},{12,10},{14,12},{11,9},... | collective-permute-start | bytes 3080 | tf_op jit(solution)/shard_map/ppermute | solution.py:31
  199.2 6.4 %collective-permute-start.5 = (f32[256]{0:T(256)S(1)}, f32[256]{0:T(256)S(1)}, u32[]{:S(2)}, u32[]{:S(2)}) collective-permute-start(f32[256]{0:T(256)S(1)} %add.226), channel_id=1, source_target_pairs={{2,0},{4,2},{6,4},{3,1},{5,3},{7,5},{10,8},{12,10},{14,12},{11,9},... | collective-permute-start | bytes 3080 | tf_op jit(solution)/shard_map/ppermute | solution.py:31
Sparse Core Ops, SparseCore 0:
  15.1 30.6 all-gather.8
  57.8 34.8 all-reduce.2
  110.7 27.9 all-gather.10
  150.8 35.0 all-reduce.4
where the time goes:
time: 220 us; the launch traced here: 219 us
  waiting for transfers between devices  84.6 us (38%)
  blocking collectives  47.4 us (22%)
  matrix products  46.8 us (21%)
  starting transfers between devices  14.5 us (7%)
  between operations  14.5 us (7%)
  local copies, waits for them, and re-layouts  5.48 us (2%)
  other arithmetic  3.67 us (2%)
    psum x2, waiting for transfers between devices, spread(): return lax.psum(kept, axis)  49 us
    all_gather x2, blocking collectives, entering(): everything = jax.tree.map(lambda part: lax.all_gather(part, axis), x)  22.7 us
    all_gather x2, waiting for transfers between devices, entering(): everything = jax.tree.map(lambda part: lax.all_gather(part, axis), x)  21.3 us
    psum x2, blocking collectives, spread(): return lax.psum(kept, axis)  20.5 us
    ppermute x6, starting transfers between devices, shifted(): lax.ppermute(value, axis, [(source, source + steps) for source in range(i...  14.3 us
    ppermute x6, waiting for transfers between devices, shifted(): lax.ppermute(value, axis, [(source, source + steps) for source in range(i...  14.2 us
    dot_general x10, matrix products, compose(): matrix = jnp.dot(later_elem[0], earlier[0], precision=highest)  12.9 us
    dot_general x10, matrix products, compose(): jnp.dot(later_elem[0], earlier[1], precision=highest) + later_elem[1]  10.4 us
  transfers between devices with their start and end apart: 10, of which 8 were waited for; matrix products, arithmetic and copies ran while one was open for 7% of the time, Pallas kernels for 0%

commit v1 on v0

--- a/solution.py
+++ b/solution.py
@@ -22,7 +22,7 @@
 
 def spread(value, axis, source):
     kept = jnp.where(lax.axis_index(axis) == source, value, 0).astype(value.dtype)
-    return lax.psum(kept, axis)
+    return jnp.sum(lax.all_gather(kept, axis), axis=0)
 
 
 def shifted(value, axis, steps):

time: 220 us -> 206 us (0.936)
  waiting for transfers between devices: 84.6 us -> 71.6 us
  other arithmetic: 3.67 us -> 6.35 us
    psum x2 -> x0, waiting for transfers between devices: 49 us -> none  [spread(): return lax.psum(kept, axis)]
    all_gather x0 -> x2, waiting for transfers between devices: none -> 34.5 us  [spread(): return jnp.sum(lax.all_gather(kept, axis), axis=0)]
    psum x2 -> x0, blocking collectives: 20.5 us -> none  [spread(): return lax.psum(kept, axis)]
    all_gather x0 -> x2, blocking collectives: none -> 18.9 us  [spread(): return jnp.sum(lax.all_gather(kept, axis), axis=0)]
    reduce_sum x0 -> x4, other arithmetic: none -> 2.68 us  [spread(): return jnp.sum(lax.all_gather(kept, axis), axis=0)]
  transfers between devices with their start and end apart: 10 -> 10, of which waited for: 8 -> 8; matrix products, arithmetic and copies ran while one was open for 7% -> 8% of each run, Pallas kernels for 0% -> 0%
where the time goes in v1:
time: 206 us; the launch traced here: 205 us
  waiting for transfers between devices  71.6 us (35%)
  blocking collectives  45.5 us (22%)
  matrix products  44.7 us (22%)
  starting transfers between devices  14.5 us (7%)
  between operations  14.4 us (7%)
  other arithmetic  6.35 us (3%)
  local copies, waits for them, and re-layouts  5.55 us (3%)
    all_gather x2, waiting for transfers between devices, spread(): return jnp.sum(lax.all_gather(kept, axis), axis=0)  34.5 us
    all_gather x2, waiting for transfers between devices, entering(): everything = jax.tree.map(lambda part: lax.all_gather(part, axis), x)  22.8 us
    all_gather x2, blocking collectives, entering(): everything = jax.tree.map(lambda part: lax.all_gather(part, axis), x)  22.3 us
    all_gather x2, blocking collectives, spread(): return jnp.sum(lax.all_gather(kept, axis), axis=0)  18.9 us
    ppermute x6, starting transfers between devices, shifted(): lax.ppermute(value, axis, [(source, source + steps) for source in range(i...  14.4 us
    ppermute x6, waiting for transfers between devices, shifted(): lax.ppermute(value, axis, [(source, source + steps) for source in range(i...  14.2 us
    dot_general x10, matrix products, compose(): matrix = jnp.dot(later_elem[0], earlier[0], precision=highest)  12.8 us
    dot_general x10, matrix products, compose(): jnp.dot(later_elem[0], earlier[1], precision=highest) + later_elem[1]  10.4 us
  transfers between devices with their start and end apart: 10, of which 8 were waited for; matrix products, arithmetic and copies ran while one was open for 8% of the time, Pallas kernels for 0%

profile of v1, /device:TPU:0, one launch (start us, length us, event | category | flops | bytes accessed | tf_op | source)
XLA Modules:
  0.0 204.6 jit_solution(11846632126981791315)
XLA Ops:
  7.2 0.6 copy-done.3
  7.9 0.7 fusion.19
  8.6 1.0 dynamic-slice_multiply_fusion
  9.6 3.1 %while.113 = (s32[]{:T(128)}, f32[256,128]{1,0:T(8,128)S(1)}, f32[8,256]{1,0:T(8,128)S(1)}, f32[256,256]{1,0:T(8,128)S(1)}, s32[]{:T(128)}, /*index=5*/s32[]{:T(128)}, s32[]{:T(128)}) while((s32[]{:T(128)}, f32[256,128]{1,0:T(8,128)S(1)}, f32[8,256]{1,0:T(8,128)S(1)}, f32[256,256]{1,0:T(8,128)S(1)}, s32[]{:T(128)}, /*index=5*/s32[]{:T(128)}, ...), condition=%wide.region_1.2_spmd, body=%wide.region_0.1_spmd.sunk | while | flops 100696064 | bytes 789627 | solution.py:56
  10.1 0.4 convolution_multiply_fusion.2
  10.5 0.4 convolution_multiply_fusion.2
  11.4 0.4 convolution_multiply_fusion.2
  11.8 0.4 convolution_multiply_fusion.2
  12.3 0.4 convolution_multiply_fusion.2
  12.7 2.3 %all_gather.54 = f32[256,256]{1,0:T(8,128)} all-gather(f32[256,128]{1,0:T(8,128)S(1)} %get-tuple-element.679), channel_id=1, replica_groups=mesh['seg'=4,'grp'=4,'pair'=2] {'pair'}, dimensions={1}, use_global_device_ids=true | all-gather | bytes 393216 | tf_op jit(solution)/shard_map/all_gather | solution.py:70
  15.0 2.9 %while.117 = (s32[]{:T(128)}, f32[256]{0:T(256)S(1)}, f32[8,256]{1,0:T(8,128)S(1)}, f32[256,256]{1,0:T(8,128)S(1)}, f32[8,256]{1,0:T(8,128)S(1)}, /*index=5*/s32[]{:T(128)}, s32[]{:T(128)}) while((s32[]{:T(128)}, f32[256]{0:T(256)S(1)}, f32[8,256]{1,0:T(8,128)S(1)}, f32[256,256]{1,0:T(8,128)S(1)}, f32[8,256]{1,0:T(8,128)S(1)}, ...), condition=%wide.region_3.4_spmd.clone, body=%wide.region_2.3_spmd.clone.sunk | while | flops 787203 | bytes 274523 | solution.py:81
  17.9 12.6 %all-gather.8 = f32[4,1,256]{2,1,0:T(1,128)S(1)} all-gather(f32[1,1,256]{2,1,0:T(1,128)S(1)} %bitcast.259), channel_id=3, replica_groups=mesh['seg'=4,'grp'=4,'pair'=2] {'seg'}, dimensions={0}, use_global_device_ids=true | all-gather | bytes 5120 | tf_op jit(solution)/shard_map/all_gather | solution.py:9
  30.6 15.1 %all-gather.17.cloned.1.call-done = f32[1024,256]{1,0:T(8,128)} async-done(((f32[256,256]{1,0:T(8,128)}), f32[1024,256]{1,0:T(8,128)}) %all-gather.17.cloned.1.call-update) | async-done | bytes 1048592 | tf_op jit(solution)/shard_map/all_gather | solution.py:9
  45.7 10.8 %while.118 = (s32[]{:T(128)}, f32[256,256]{1,0:T(8,128)S(1)}, f32[256]{0:T(256)S(1)}, s32[]{:T(128)}, f32[4,256,256]{2,1,0:T(8,128)}, /*index=5*/f32[4,256]{1,0:T(4,128)S(1)}, s32[]{:T(128)}, s32[]{:T(128)}) while((s32[]{:T(128)}, f32[256,256]{1,0:T(8,128)S(1)}, f32[256]{0:T(256)S(1)}, s32[]{:T(128)}, f32[4,256,256]{2,1,0:T(8,128)}, ...), condition=%wide.region_5.6_spmd.clone, body=%wide.region_4.5_spmd.clone.sunk | while | flops 202179584 | bytes 1846383 | solution.py:20
  45.7 1.3 fusion.140
  47.1 1.3 convolution_select_fusion.6
  48.5 1.2 fusion.140
  49.8 1.3 convolution_select_fusion.6
  51.2 1.2 fusion.140
  52.5 1.3 convolution_select_fusion.6
  53.9 1.2 fusion.140
  55.2 1.3 convolution_select_fusion.6
  56.6 1.1 convolution_select_fusion.3
  57.9 0.7 copy-done.4
  59.1 9.4 %all-gather.9 = f32[4,1,256]{2,1,0:T(1,128)S(1)} all-gather(f32[1,1,256]{2,1,0:T(1,128)S(1)} %bitcast.284), channel_id=5, replica_groups=mesh['seg'=4,'grp'=4,'pair'=2] {'seg'}, dimensions={0}, use_global_device_ids=true | all-gather | bytes 5120 | tf_op jit(solution)/shard_map/all_gather | solution.py:25
  68.5 16.7 %all-gather.19.cloned.1.call-done = f32[1024,256]{1,0:T(8,128)} async-done(((f32[256,256]{1,0:T(8,128)}), f32[1024,256]{1,0:T(8,128)}) %all-gather.19.cloned.1.call-update) | async-done | bytes 1048592 | tf_op jit(solution)/shard_map/all_gather | solution.py:25
  85.2 1.3 reduce_sum.36
  86.6 0.7 copy-done.5
  87.5 3.4 %collective-permute-start = (f32[256]{0:T(256)S(1)}, f32[256]{0:T(256)S(1)}, u32[]{:S(2)}, u32[]{:S(2)}) collective-permute-start(f32[256]{0:T(256)S(1)} %add.210), channel_id=1, source_target_pairs={{0,2},{2,4},{4,6},{1,3},{3,5},{5,7},{8,10},{10,12},{12,14},{9,11},... | collective-permute-start | bytes 3080 | tf_op jit(solution)/shard_map/ppermute | solution.py:31
  90.9 2.9 %while.115 = (s32[]{:T(128)}, f32[256,128]{1,0:T(8,128)S(1)}, f32[256,256]{1,0:T(8,128)S(1)}, s32[]{:T(128)}) while((s32[]{:T(128)}, f32[256,128]{1,0:T(8,128)S(1)}, f32[256,256]{1,0:T(8,128)S(1)}, s32[]{:T(128)}) %tuple.227), condition=%wide.region_11.12_spmd, body=%wide.region_10.11_spmd.sunk | while | flops 100663296 | bytes 786485 | solution.py:66
  91.0 0.4 fusion.126
  92.2 0.4 fusion.126
  92.6 0.4 fusion.126
  93.5 0.4 fusion.126
  94.2 3.4 %collective-permute-start.1 = (f32[256]{0:T(256)S(1)}, f32[256]{0:T(256)S(1)}, u32[]{:S(2)}, u32[]{:S(2)}) collective-permute-start(f32[256]{0:T(256)S(1)} %add.211), channel_id=1, source_target_pairs={{0,2},{2,4},{4,6},{1,3},{3,5},{5,7},{8,10},{10,12},{12,14},{9,11},... | collective-permute-start | bytes 3080 | tf_op jit(solution)/shard_map/ppermute | solution.py:31
  97.6 2.0 all_gather.63
  99.9 3.5 %collective-permute-start.2 = (f32[256]{0:T(256)S(1)}, f32[256]{0:T(256)S(1)}, u32[]{:S(2)}, u32[]{:S(2)}) collective-permute-start(f32[256]{0:T(256)S(1)} %add.212), channel_id=1, source_target_pairs={{0,2},{2,4},{4,6},{1,3},{3,5},{5,7},{8,10},{10,12},{12,14},{9,11},... | collective-permute-start | bytes 3080 | tf_op jit(solution)/shard_map/ppermute | solution.py:31
  103.4 0.7 broadcast_select_fusion.3
  104.2 0.5 collective-permute-done.2
  105.0 3.2 %while.114 = (s32[]{:T(128)}, f32[256]{0:T(256)S(1)}, f32[8,256]{1,0:T(8,128)S(1)}, f32[8,256]{1,0:T(8,128)S(1)}, f32[256,256]{1,0:T(8,128)S(1)}, /*index=5*/f32[8,256]{1,0:T(8,128)S(1)}, s32[]{:T(128)}, s32[]{:T(128)}) while((s32[]{:T(128)}, f32[256]{0:T(256)S(1)}, f32[8,256]{1,0:T(8,128)S(1)}, f32[8,256]{1,0:T(8,128)S(1)}, ...), condition=%wide.region_9.10_spmd, body=%wide.region_8.9_spmd.sunk | while | flops 786946 | bytes 274525 | solution.py:81
  108.2 5.3 %while.119 = (s32[]{:T(128)}, f32[256]{0:T(256)S(1)}, f32[8,256]{1,0:T(8,128)S(1)}, f32[256,256]{1,0:T(8,128)S(1)}, f32[256,256]{1,0:T(8,128)S(1)}, /*index=5*/s32[]{:T(128)}, s32[]{:T(128)}, s32[]{:T(128)}) while((s32[]{:T(128)}, f32[256]{0:T(256)S(1)}, f32[8,256]{1,0:T(8,128)S(1)}, f32[256,256]{1,0:T(8,128)S(1)}, ...), condition=%wide.region_13.14_spmd.clone, body=%wide.region_12.13_spmd.clone.sunk | while | flops 1573636 | bytes 536687 | solution.py:92
  114.2 9.7 %all-gather.10 = f32[4,1,256]{2,1,0:T(1,128)S(1)} all-gather(f32[1,1,256]{2,1,0:T(1,128)S(1)} %bitcast.266), channel_id=7, replica_groups=mesh['seg'=4,'grp'=4,'pair'=2] {'seg'}, dimensions={0}, use_global_device_ids=true | all-gather | bytes 5120 | tf_op jit(solution)/shard_map/all_gather | solution.py:9
  123.9 7.7 %all-gather.21.cloned.1.call-done = f32[1024,256]{1,0:T(8,128)} async-done(((f32[256,256]{1,0:T(8,128)}), f32[1024,256]{1,0:T(8,128)}) %all-gather.21.cloned.1.call-update) | async-done | bytes 1048592 | tf_op jit(solution)/shard_map/all_gather | solution.py:9
  131.6 10.9 %while.120 = (s32[]{:T(128)}, f32[256,256]{1,0:T(8,128)S(1)}, f32[256]{0:T(256)S(1)}, s32[]{:T(128)}, f32[4,256,256]{2,1,0:T(8,128)}, /*index=5*/f32[4,256]{1,0:...) while((s32[]{:T(128)}, f32[256,256]{1,0:T(8,128)S(1)}, f32[256]{0:T(256)S(1)}, ...), condition=%wide.region_15.16_spmd.clone, body=%wide.region_14.15_spmd.clone.sunk | while | flops 202179584 | bytes 1845429 | solution.py:20
  131.6 1.3 fusion.151
  133.0 1.3 convolution_select_fusion.7
  134.4 1.2 fusion.151
  135.7 1.3 convolution_select_fusion.7
  137.1 1.2 fusion.151
  138.5 1.3 convolution_select_fusion.7
  139.8 1.2 fusion.151
  141.2 1.3 convolution_select_fusion.7
  142.5 1.1 convolution_select_fusion.2
  144.0 9.5 %all-gather.11 = f32[4,1,256]{2,1,0:T(1,128)S(1)} all-gather(f32[1,1,256]{2,1,0:T(1,128)S(1)} %bitcast.283), channel_id=9, replica_groups=mesh['seg'=4,'grp'=4,'pair'=2] {'seg'}, dimensions={0}, use_global_device_ids=true | all-gather | bytes 5120 | tf_op jit(solution)/shard_map/all_gather | solution.py:25
  153.5 17.8 %all-gather.23.cloned.1.call-done = f32[1024,256]{1,0:T(8,128)} async-done(((f32[256,256]{1,0:T(8,128)}), f32[1024,256]{1,0:T(8,128)}) %all-gather.23.cloned.1.call-update) | async-done | bytes 1048592 | tf_op jit(solution)/shard_map/all_gather | solution.py:25
  171.3 1.3 reduce_sum.38
  172.9 1.3 collective-permute-start.3
  174.3 4.2 %collective-permute-done.3 = f32[256]{0:T(256)S(1)} collective-permute-done((f32[256]{0:T(256)S(1)}, f32[256]{0:T(256)S(1)}, u32[]{:S(2)}, u32[]{:S(2)}) %collective-permute-start.3) | collective-permute-done | bytes 1056 | tf_op jit(solution)/shard_map/ppermute | solution.py:31
  178.7 1.3 collective-permute-start.4
  180.1 4.5 %collective-permute-done.4 = f32[256]{0:T(256)S(1)} collective-permute-done((f32[256]{0:T(256)S(1)}, f32[256]{0:T(256)S(1)}, u32[]{:S(2)}, u32[]{:S(2)}) %collective-permute-start.4) | collective-permute-done | bytes 1056 | tf_op jit(solution)/shard_map/ppermute | solution.py:31
  184.9 1.3 collective-permute-start.5
  186.2 5.1 %collective-permute-done.5 = f32[256]{0:T(256)S(1)} collective-permute-done((f32[256]{0:T(256)S(1)}, f32[256]{0:T(256)S(1)}, u32[]{:S(2)}, u32[]{:S(2)}) %collective-permute-start.5) | collective-permute-done | bytes 1056 | tf_op jit(solution)/shard_map/ppermute | solution.py:31
  191.6 5.8 %while.116 = (s32[]{:T(128)}, f32[256]{0:T(256)S(1)}, f32[8,256]{1,0:T(8,128)S(1)}, f32[8,256]{1,0:T(8,128)S(1)}, f32[256,256]{1,0:T(8,128)S(1)}, /*index=5*/f32...) while((s32[]{:T(128)}, f32[256]{0:T(256)S(1)}, f32[8,256]{1,0:T(8,128)S(1)}, f32[8,256]{1,0:T(8,128)S(1)}, ...), condition=%wide.region_19.20_spmd, body=%wide.region_18.19_spmd.sunk | while | flops 1573379 | bytes 538737 | solution.py:92
  197.4 0.6 constant_dynamic-slice_fusion.9
  (275 shorter events, 23.1 us)
Async XLA Ops:
  7.2 0.7 copy-start.3
  7.2 2.4 %copy-start = (f32[256,256]{1,0:T(8,128)S(1)}, f32[256,256]{1,0:T(8,128)}, u32[]{:S(2)}) copy-start(f32[256,256]{1,0:T(8,128)} %param.25) | copy-start | bytes 786436
  7.2 38.5 %all-gather.17.cloned.1.call-start = ((), (), s32[]{:S(2)}) async-start(), calls=%async_computation | async-start | bytes 1310720 | tf_op jit(solution)/shard_map/all_gather | solution.py:9
  14.9 70.3 %all-gather.19.cloned.1.call-start = ((), (), s32[]{:S(2)}) async-start(), calls=%async_computation.1 | async-start | bytes 1310720 | tf_op jit(solution)/shard_map/all_gather | solution.py:25
  45.7 10.8 %copy-start.2 = (f32[256,256]{1,0:T(8,128)S(1)}, f32[256,256]{1,0:T(8,128)}, u32[]{:S(2)}) copy-start(f32[256,256]{1,0:T(8,128)} %all_gather.54) | copy-start | bytes 786436
  57.7 73.9 %all-gather.21.cloned.1.call-start = ((), (), s32[]{:S(2)}) async-start(), calls=%async_computation.2 | async-start | bytes 1310720 | tf_op jit(solution)/shard_map/all_gather | solution.py:9
  57.9 0.7 copy-start.4
  86.6 0.7 copy-start.5
  87.5 6.3 %collective-permute-start = (f32[256]{0:T(256)S(1)}, f32[256]{0:T(256)S(1)}, u32[]{:S(2)}, u32[]{:S(2)}) collective-permute-start(f32[256]{0:T(256)S(1)} %add.210), channel_id=1, source_target_pairs={{0,2},{2,4},{4,6},{1,3},{3,5},{5,7},{8,10},{10,12},{12,14},{9,11},... | collective-permute-start | bytes 3080 | tf_op jit(solution)/shard_map/ppermute | solution.py:31
  94.2 5.4 %collective-permute-start.1 = (f32[256]{0:T(256)S(1)}, f32[256]{0:T(256)S(1)}, u32[]{:S(2)}, u32[]{:S(2)}) collective-permute-start(f32[256]{0:T(256)S(1)} %add.211), channel_id=1, source_target_pairs={{0,2},{2,4},{4,6},{1,3},{3,5},{5,7},{8,10},{10,12},{12,14},{9,11},... | collective-permute-start | bytes 3080 | tf_op jit(solution)/shard_map/ppermute | solution.py:31
  99.9 4.8 %collective-permute-start.2 = (f32[256]{0:T(256)S(1)}, f32[256]{0:T(256)S(1)}, u32[]{:S(2)}, u32[]{:S(2)}) collective-permute-start(f32[256]{0:T(256)S(1)} %add.212), channel_id=1, source_target_pairs={{0,2},{2,4},{4,6},{1,3},{3,5},{5,7},{8,10},{10,12},{12,14},{9,11},... | collective-permute-start | bytes 3080 | tf_op jit(solution)/shard_map/ppermute | solution.py:31
  104.1 67.2 %all-gather.23.cloned.1.call-start = ((), (), s32[]{:S(2)}) async-start(), calls=%async_computation.3 | async-start | bytes 1310720 | tf_op jit(solution)/shard_map/all_gather | solution.py:25
  131.6 10.9 %copy-start.1 = (f32[256,256]{1,0:T(8,128)S(1)}, f32[256,256]{1,0:T(8,128)}, u32[]{:S(2)}) copy-start(f32[256,256]{1,0:T(8,128)} %broadcast_select_fusion.3) | copy-start | bytes 786436
  172.9 5.5 %collective-permute-start.3 = (f32[256]{0:T(256)S(1)}, f32[256]{0:T(256)S(1)}, u32[]{:S(2)}, u32[]{:S(2)}) collective-permute-start(f32[256]{0:T(256)S(1)} %add.216), channel_id=1, source_target_pairs={{2,0},{4,2},{6,4},{3,1},{5,3},{7,5},{10,8},{12,10},{14,12},{11,9},... | collective-permute-start | bytes 3080 | tf_op jit(solution)/shard_map/ppermute | solution.py:31
  178.7 5.9 %collective-permute-start.4 = (f32[256]{0:T(256)S(1)}, f32[256]{0:T(256)S(1)}, u32[]{:S(2)}, u32[]{:S(2)}) collective-permute-start(f32[256]{0:T(256)S(1)} %add.217), channel_id=1, source_target_pairs={{2,0},{4,2},{6,4},{3,1},{5,3},{7,5},{10,8},{12,10},{14,12},{11,9},... | collective-permute-start | bytes 3080 | tf_op jit(solution)/shard_map/ppermute | solution.py:31
  184.9 6.4 %collective-permute-start.5 = (f32[256]{0:T(256)S(1)}, f32[256]{0:T(256)S(1)}, u32[]{:S(2)}, u32[]{:S(2)}) collective-permute-start(f32[256]{0:T(256)S(1)} %add.218), channel_id=1, source_target_pairs={{2,0},{4,2},{6,4},{3,1},{5,3},{7,5},{10,8},{12,10},{14,12},{11,9},... | collective-permute-start | bytes 3080 | tf_op jit(solution)/shard_map/ppermute | solution.py:31
Sparse Core Ops, SparseCore 0:
  15.1 30.6 all-gather.16
  57.8 27.3 all-gather.18
  104.3 27.3 all-gather.20
  143.8 27.5 all-gather.22
